TPU v7x, 32 devices: a whole 2x2x4 slice. The times are simulated.
32 devices in a mesh: grp: 2 (over x), region: 8 (over z, y), donor: 2 (over core).
Axes of the slice: x: 2, y: 2, z: 4, core: 2. Of those that a mesh axis runs over, the one named last changes fastest.
Arguments:
- dosage: bfloat16 [16384, 8192], P(('grp', 'region'), 'donor'), parts along dimension 0, may hold values from 0 to 2, as said below
- expression: bfloat16 [512, 8192], P(('grp', 'region'), 'donor'), parts along dimension 0, may hold values from -60 to 60
- cis_tiles: int32 [512, 8], P(('grp', 'region')), parts along dimension 0, may hold values from 0 to 63, as said below
Outputs:
- correlation: float32 [512, 1024], P(('grp', 'region'), 'donor'), parts along dimension 0
- pvalue: float32 [512, 1024], P(('grp', 'region'), 'donor'), parts along dimension 0
There are 2 independent parts, one for each index of `grp`. A program takes and returns all parts, laid end to end along the dimension named above; each array names one. Nothing has to cross between parts.
Inputs may be any that keep to these rules, and one draw needn't show every extreme that they name: `dosage`: imputed dosages, within the bounds. `cis_tiles`: each gene's 8 cis tiles are consecutive tile numbers; for the genes of region block r (rows r * 32 to (r + 1) * 32 - 1) they lie from r * 8 - 8 to (r + 1) * 8 + 7, and both ends are reached in every block where they exist.
All inputs are finite; a program needn't handle non-finite values.
Results may differ from a plain program's by a relative error of at most 0.0044.
Values may be sent and summed in bfloat16 or wider, within the bound.
A program may use at most 128 MiB of HBM per device.

v0:
```python
import math

import jax
import jax.numpy as jnp
from jax import lax
from jax.sharding import PartitionSpec as P

TILE = 128
RIM = 8
CF_TERMS = 32


def with_halo(array, sides, width):
    for axis, dim in sides:
        count, length = (lax.axis_size(axis), array.shape[dim])
        up = [(i, (i + 1) % count) for i in range(count - 1)]
        down = [(j, i) for i, j in up]
        last = lax.slice_in_dim(array, length - width, length, axis=dim)
        leading = lax.slice_in_dim(array, 0, width, axis=dim)
        before = lax.ppermute(last, axis, up)
        after = lax.ppermute(leading, axis, down)
        array = jnp.concatenate([before, array, after], axis=dim)
    return array


def beta_log_constant(shape_a):
    inverse = 1.0 / shape_a
    ratio = (
        0.5 * math.log(shape_a)
        - inverse / 8.0
        + inverse**3 / 192.0
        + inverse**5 / 640.0
        - 17.0 * inverse**7 / 14336.0
    )
    return ratio - 0.5 * math.log(math.pi)


def scale_rows(values, totals, squares, count):
    center = totals / count
    spread = squares / count - center * center
    return (
        (values.astype(jnp.float32) - center[:, None]) * lax.rsqrt(spread + 1e-05)[:, None]
    ).astype(jnp.bfloat16)


def donor_product(left_rows, right_rows):
    return lax.dot_general(
        left_rows, right_rows, (((1,), (1,)), ((), ())), preferred_element_type=jnp.float32
    )


def tail_probability(squared, shape_a, log_const, terms):
    narrow = squared < 1.5 / (shape_a + 2.5)
    first = jnp.where(narrow, 0.5, shape_a)
    second = jnp.where(narrow, shape_a, 0.5)
    argument = jnp.where(narrow, squared, 1.0 - squared)
    total_ab = first + second

    def odd_term(index):
        return (
            -(first + index)
            * (total_ab + index)
            * argument
            / ((first + 2.0 * index) * (first + 2.0 * index + 1.0))
        )

    def even_term(index):
        return (
            index
            * (second - index)
            * argument
            / ((first + 2.0 * index - 1.0) * (first + 2.0 * index))
        )

    def advance(carried, coefficient):
        upper_ratio, lower_ratio, estimate = carried
        lower_ratio = 1.0 / (1.0 + coefficient * lower_ratio)
        upper_ratio = 1.0 + coefficient / upper_ratio
        return (upper_ratio, lower_ratio, estimate * lower_ratio * upper_ratio)

    def sweep(turn, carried):
        for offset in range(4):
            index = (4 * turn + offset + 1).astype(jnp.float32)
            carried = advance(carried, even_term(index))
            carried = advance(carried, odd_term(index))
        return carried

    leading = 1.0 / (1.0 - total_ab * argument / (first + 1.0))
    start = (jnp.ones_like(squared), leading, leading)
    carried = lax.fori_loop(0, terms // 4, sweep, start)
    estimate = carried[2]
    front = jnp.sqrt(squared) * jnp.exp(shape_a * jnp.log1p(-squared) + log_const)
    share = front * estimate / first
    return jnp.where(narrow, 1.0 - share, share)


def shards(dosage, expression, cis_tiles):
    donor_total = dosage.shape[1] * lax.axis_size("donor")
    gene_count = expression.shape[0]
    block_tiles = dosage.shape[0] // TILE
    rim_rows = RIM * TILE
    dose_total = jnp.sum(dosage, axis=1, dtype=jnp.float32)
    dose_square = jnp.sum(jnp.square(dosage.astype(jnp.float32)), axis=1)
    expr_total = jnp.sum(expression, axis=1, dtype=jnp.float32)
    expr_square = jnp.sum(jnp.square(expression.astype(jnp.float32)), axis=1)
    moments = lax.psum((dose_total, dose_square, expr_total, expr_square), "donor")
    zdose = scale_rows(dosage, moments[0], moments[1], donor_total)
    zexpr = scale_rows(expression, moments[2], moments[3], donor_total)
    widened = with_halo(zdose, (("region", 0),), rim_rows)
    dense = donor_product(zexpr, widened)
    first_tile = lax.axis_index("region") * block_tiles - RIM
    local_tile = cis_tiles - first_tile
    layered = dense.reshape(gene_count, block_tiles + 2 * RIM, TILE)
    index_grid = jnp.broadcast_to(local_tile[:, :, None], (gene_count, local_tile.shape[1], TILE))
    picked = jnp.take_along_axis(layered, index_grid, axis=1)
    partial_pairs = picked.reshape(gene_count, local_tile.shape[1] * TILE)
    share_width = partial_pairs.shape[1] // lax.axis_size("donor")
    summed = lax.psum(partial_pairs, "donor")
    own_pairs = lax.dynamic_slice_in_dim(
        summed, lax.axis_index("donor") * share_width, share_width, 1
    )
    correlation = own_pairs / donor_total
    squared = jnp.minimum(correlation * correlation, 0.9)
    shape_a = (donor_total - 2) / 2.0
    log_const = beta_log_constant(shape_a)
    pvalue = tail_probability(squared, shape_a, log_const, CF_TERMS)
    return (correlation, pvalue)


def solution(mesh):
    in_specs = (
        P(("grp", "region"), "donor"),
        P(("grp", "region"), "donor"),
        P(("grp", "region"), None),
    )
    out_specs = (P(("grp", "region"), "donor"), P(("grp", "region"), "donor"))
    return jax.shard_map(shards, mesh=mesh, in_specs=in_specs, out_specs=out_specs, check_vma=False)
```

profile of v0, /device:TPU:9, one launch (start us, length us, event | category | flops | bytes accessed | tf_op | source)
XLA Modules:
  0.0 695.0 jit_solution(16506730900923522625)
XLA Ops:
  7.2 0.0 copy-start.1
  7.2 0.0 all-reduce.3.cloned.1.call-start
  7.2 6.0 convert_reduce_fusion
  13.2 0.0 copy-done.1
  13.2 0.2 convert_reduce_fusion.1
  13.4 2.8 all-reduce
  16.2 0.0 copy-start.2
  16.3 11.0 %fusion.9 = bf16[1024,4096]{1,0:T(8,128)(2,1)} fusion(bf16[1024,4096]{1,0:T(8,128)(2,1)} %param.5, f32[1024]{0:T(1024)S(1)} %get-tuple-element.298, f32[1024]{0:T(1024)S(1)} %get-tuple-element.297), kind=kLoop, calls=%fused_computation.46 | loop fusion | flops 16777216 | bytes 16785408 | tf_op jit(solution)/shard_map/convert_element_type | solution.py:43
  27.3 3.1 collective-permute-start
  30.4 3.0 collective-permute-start.1
  33.5 0.0 copy-done.2
  33.5 0.1 copy.13
  33.6 0.1 copy.12
  33.7 0.1 copy.11
  33.8 0.2 or_bitcast_fusion
  34.0 356.0 %collective-permute-done = bf16[1024,4096]{1,0:T(8,128)(2,1)} collective-permute-done((bf16[1024,4096]{1,0:T(8,128)(2,1)}, bf16[1024,4096]{1,0:T(8,128)(2,1)}, u32[]{:S(2)}, u32[]{:S(2)}) %collective-permute-start) | collective-permute-done | bytes 8388640 | tf_op jit(solution)/shard_map/ppermute | solution.py:20
  390.0 2.5 collective-permute-done.1
  392.5 11.8 %fusion.11 = f32[4,8,24,128]{3,1,2,0:T(8,128)S(1)} fusion(bf16[1024,4096]{1,0:T(8,128)(2,1)} %collective-permute-done.1, bf16[1024,4096]{1,0:T(8,128)(2,1)} %fusion.9, bf16[1024,4096]{1,0:T(8,128)(2,1)} %collective-permute-done, bf16[32,4096]{1,0:T(8,128)(2,1)S(1)} %copy-done.1, f32[32]{0:T(128)S(1)} %get-tuple-element.300, f32[32]{0:T(128)S(1)} %get-tuple-element.299), kind=kOutput, calls=%fused_computation.48 | convolution fusion | flops 881328128 | bytes 25821440 | tf_op jit(solution)/shard_map/dot_general | solution.py:47
  404.4 0.1 copy.17
  404.4 259.4 %gather_fusion = f32[32768]{0:T(1024)S(1)} fusion(f32[32,24,128]{2,1,0:T(8,128)S(1)} %bitcast.11, s32[32768]{0:T(1024)S(1)} %or_bitcast_fusion), kind=kCustom, calls=%fused_computation | custom fusion | bytes 655360 | tf_op jit(solution)/shard_map/jit(take_along_axis)/gather | solution.py:115
  663.8 0.2 bitcast_select_fusion
  664.0 0.7 copy.20
  664.7 0.0 all-reduce.3.cloned.1.call-update
  664.7 18.8 %all-reduce.3.cloned.1.call-done = f32[32,1024]{1,0:T(8,128)} async-done(((f32[32,1024]{1,0:T(8,128)}), f32[32,1024]{1,0:T(8,128)}) %all-reduce.3.cloned.1.call-update) | async-done | bytes 131088 | tf_op jit(solution)/shard_map/psum | solution.py:118
  683.5 0.9 broadcast_select_fusion
  684.4 0.0 copy-start
  684.5 3.0 while.21
  684.5 0.3 multiply_multiply_fusion.10
  684.8 0.3 multiply_multiply_fusion.10
  685.2 0.3 multiply_multiply_fusion.10
  685.6 0.3 multiply_multiply_fusion.10
  686.0 0.3 multiply_multiply_fusion.10
  686.3 0.3 multiply_multiply_fusion.10
  686.7 0.3 multiply_multiply_fusion.10
  687.1 0.3 multiply_multiply_fusion.10
  687.4 0.7 subtract_select_fusion
  688.1 0.0 copy-done
  (7 shorter events, 0.1 us)
Async XLA Ops:
  7.2 6.0 copy-start.1
  7.2 676.3 %all-reduce.3.cloned.1.call-start = ((), (), s32[]{:S(2)}) async-start(), calls=%async_computation | async-start | bytes 262144 | tf_op jit(solution)/shard_map/psum | solution.py:118
  16.2 17.2 %copy-start.2 = (s32[32,8]{0,1:T(8,128)S(1)}, s32[32,8]{0,1:T(8,128)}, u32[]{:S(2)}) copy-start(s32[32,8]{0,1:T(8,128)} %param.7) | copy-start | bytes 3076
  27.3 362.7 %collective-permute-start = (bf16[1024,4096]{1,0:T(8,128)(2,1)}, bf16[1024,4096]{1,0:T(8,128)(2,1)}, u32[]{:S(2)}, u32[]{:S(2)}) collective-permute-start(bf16[1024,4096]{1,0:T(8,128)(2,1)} %fusion.9), channel_id=1, source_target_pairs={{0,2},{2,4},{4,6},{6,8},{8,10},{10,12},{12,14},{1,3},{3,5},{5,7},{... | collective-permute-start | bytes 25165832 | tf_op jit(solution)/shard_map/ppermute | solution.py:20
  30.4 362.1 %collective-permute-start.1 = (bf16[1024,4096]{1,0:T(8,128)(2,1)}, bf16[1024,4096]{1,0:T(8,128)(2,1)}, u32[]{:S(2)}, u32[]{:S(2)}) collective-permute-start(bf16[1024,4096]{1,0:T(8,128)(2,1)} %fusion.9), channel_id=1, source_target_pairs={{2,0},{4,2},{6,4},{8,6},{10,8},{12,10},{14,12},{3,1},{5,3},{7,5},{... | collective-permute-start | bytes 25165832 | tf_op jit(solution)/shard_map/ppermute | solution.py:21
  684.4 3.8 copy-start
Sparse Core Ops, SparseCore 0:
  664.8 18.6 all-reduce.2
where the time goes:
time: 696 us; the launch traced here: 695 us
  waiting for transfers between devices  377 us (54%)
  local copies, waits for them, and re-layouts  260 us (37%)
  other arithmetic  21.9 us (3%)
  between operations  14.2 us (2%)
  matrix products  11.8 us (2%)
    ppermute x1, waiting for transfers between devices, with_halo(): before = lax.ppermute(last, axis, up)  356 us
    gather x1, local copies, waits for them, and re-layouts, shards(): picked = jnp.take_along_axis(layered, index_grid, axis=1)  259 us
    psum x1, waiting for transfers between devices, shards(): summed = lax.psum(partial_pairs, 'donor')  18.8 us
  transfers between devices with their start and end apart: 3, of which 3 were waited for; matrix products, arithmetic and copies ran while one was open for 0% of the time, Pallas kernels for 0%

commit v1 on v0

v1 whole, which is shorter than its diff:
```python
import functools
import math

import jax
import jax.numpy as jnp
from jax import lax
from jax.experimental import pallas as pl
from jax.experimental.pallas import tpu as pltpu
from jax.sharding import PartitionSpec as P

TILE = 128
CF_TERMS = 32
CHUNKS = 4
ROWS = 256
MESH = pl.DeviceIdType.MESH


def beta_log_constant(shape_a):
    inverse = 1.0 / shape_a
    ratio = (
        0.5 * math.log(shape_a)
        - inverse / 8.0
        + inverse**3 / 192.0
        + inverse**5 / 640.0
        - 17.0 * inverse**7 / 14336.0
    )
    return ratio - 0.5 * math.log(math.pi)


def coefficients(a, b, terms):
    out = [-(a + b) / (a + 1.0)]
    for m in range(1, terms + 1):
        out.append(m * (b - m) / ((a + 2.0 * m - 1.0) * (a + 2.0 * m)))
        out.append(-(a + m) * (a + b + m) / ((a + 2.0 * m) * (a + 2.0 * m + 1.0)))
    return out


def tail_probability(squared, shape_a, log_const, terms):
    narrow = squared < 1.5 / (shape_a + 2.5)
    argument = jnp.where(narrow, squared, 1.0 - squared)
    small = coefficients(0.5, shape_a, terms)
    large = coefficients(shape_a, 0.5, terms)
    level = jnp.ones_like(squared)
    for c_small, c_large in zip(small[::-1], large[::-1]):
        level = 1.0 + jnp.where(narrow, c_small, c_large) * argument / level
    front = jnp.sqrt(squared) * jnp.exp(shape_a * jnp.log1p(-squared) + log_const)
    share = front / (level * jnp.where(narrow, 0.5, shape_a))
    return jnp.where(narrow, 1.0 - share, share)


def lane_sums(block_of, columns, rows):
    total = jnp.zeros((rows, 128), jnp.float32)
    square = jnp.zeros((rows, 128), jnp.float32)
    for j in range(columns // 128):
        x = block_of(j).astype(jnp.float32)
        total = total + x
        square = square + x * x
    return total, square


def dot_t(left, right):
    return lax.dot_general(
        left, right, (((1,), (1,)), ((), ())), preferred_element_type=jnp.float32
    )


def kernel(
    sizes,
    dose_hbm, expr_ref, cis_ref,
    corr_ref, pval_ref,
    dose, zown, zin, cin, mom, mom_in, acc, dstat, dstat_in, prod,
    sel_own, own_in, sel_nbr, nbr_in, ret, ret_in,
    dose_sem, z_send, z_recv, c_send, c_recv, s_send, s_recv, r_send, r_recv,
):
    genes, local, variants, regions, donors = sizes
    tiles = variants // TILE
    width = local // CHUNKS
    half = corr_ref.shape[1]
    half_k = half // TILE
    me = lax.axis_index("region")
    core = lax.axis_index("donor")
    has_prev = me > 0
    has_next = me < regions - 1
    prev = jnp.maximum(me - 1, 0)
    nxt = jnp.minimum(me + 1, regions - 1)
    sibling = {"donor": 1 - core}
    sides = ((0, has_prev, {"region": prev}), (1, has_next, {"region": nxt}))

    barrier = pltpu.get_barrier_semaphore()
    pl.semaphore_signal(barrier, inc=1, device_id=sibling, device_id_type=MESH)
    for _, there, where in sides:
        @pl.when(there)
        def _():
            pl.semaphore_signal(barrier, inc=1, device_id=where, device_id_type=MESH)

    blocks = variants // ROWS
    loads = [
        pltpu.make_async_copy(
            dose_hbm.at[pl.ds(i * ROWS, ROWS)], dose.at[pl.ds(i * ROWS, ROWS)], dose_sem.at[i]
        )
        for i in range(blocks)
    ]
    for load in loads:
        load.start()

    total, square = lane_sums(lambda j: expr_ref[:, j * 128:(j + 1) * 128], local, genes)
    total = jnp.sum(total, axis=1, keepdims=True)
    square = jnp.sum(square, axis=1, keepdims=True)
    lane = lax.broadcasted_iota(jnp.int32, (genes, 128), 1)
    mom[...] = jnp.where(lane == 0, total, square)
    for side in range(2):
        @pl.when(jnp.logical_not(sides[side][1]))
        def _():
            zin[:, pl.ds(side * genes, genes), :] = jnp.zeros((CHUNKS, genes, width), jnp.bfloat16)
            cin[side] = jnp.zeros(cis_ref.shape, jnp.int32)

    pl.semaphore_wait(barrier, 1 + has_prev.astype(jnp.int32) + has_next.astype(jnp.int32))

    def to_sibling(src, dst, slot):
        return pltpu.make_async_remote_copy(
            src_ref=src, dst_ref=dst, send_sem=s_send.at[slot], recv_sem=s_recv.at[slot],
            device_id=sibling, device_id_type=MESH,
        )

    mom_copy = to_sibling(mom, mom_in, 0)
    mom_copy.start()

    def cis_copy(side):
        return pltpu.make_async_remote_copy(
            src_ref=cis_ref, dst_ref=cin.at[1 - side], send_sem=c_send.at[side],
            recv_sem=c_recv.at[1 - side], device_id=sides[side][2], device_id_type=MESH,
        )

    def z_copy(side, j):
        return pltpu.make_async_remote_copy(
            src_ref=zown.at[j], dst_ref=zin.at[j, pl.ds((1 - side) * genes, genes)],
            send_sem=z_send.at[side, j], recv_sem=z_recv.at[1 - side, j],
            device_id=sides[side][2], device_id_type=MESH,
        )

    def z_arrival(side, j):
        return pltpu.make_async_remote_copy(
            src_ref=zown.at[j], dst_ref=zin.at[j, pl.ds(side * genes, genes)],
            send_sem=z_send.at[side, j], recv_sem=z_recv.at[side, j],
            device_id=sides[side][2], device_id_type=MESH,
        )

    def cis_arrival(side):
        return pltpu.make_async_remote_copy(
            src_ref=cis_ref, dst_ref=cin.at[side], send_sem=c_send.at[side],
            recv_sem=c_recv.at[side], device_id=sides[side][2], device_id_type=MESH,
        )

    def ret_copy(side):
        return pltpu.make_async_remote_copy(
            src_ref=ret.at[pl.ds(side * genes, genes)], dst_ref=ret_in.at[1 - side],
            send_sem=r_send.at[side], recv_sem=r_recv.at[1 - side],
            device_id=sides[side][2], device_id_type=MESH,
        )

    def ret_arrival(side):
        return pltpu.make_async_remote_copy(
            src_ref=ret.at[pl.ds(side * genes, genes)], dst_ref=ret_in.at[side],
            send_sem=r_send.at[side], recv_sem=r_recv.at[side],
            device_id=sides[side][2], device_id_type=MESH,
        )

    mom_copy.wait_recv()
    sums = mom[...] + mom_in[...]
    center = sums[:, 0:1] / donors
    spread = sums[:, 1:2] / donors - center * center
    scale = lax.rsqrt(spread + 1e-05)
    z_sum = jnp.zeros((genes, 1), jnp.float32)
    for j in range(CHUNKS):
        y = expr_ref[:, j * width:(j + 1) * width].astype(jnp.float32)
        z = ((y - center) * scale).astype(jnp.bfloat16)
        zown[j] = z
        for side, there, _ in sides:
            @pl.when(there)
            def _():
                z_copy(side, j).start()
        z_sum = z_sum + jnp.sum(z.astype(jnp.float32), axis=1, keepdims=True)
    for side, there, _ in sides:
        @pl.when(there)
        def _():
            cis_copy(side).start()

    group = 32
    for i in range(blocks):
        loads[i].wait()

        def row_group(q, carry):
            start = pl.multiple_of(i * ROWS + q * group, group)
            rows = pl.ds(start, group)
            t, s = lane_sums(lambda j: dose[rows, j * 128:(j + 1) * 128], local, group)
            acc[0, rows] = t
            acc[1, rows] = s
            return carry

        lax.fori_loop(0, ROWS // group, row_group, 0)
        for w in range(2):
            for h in range(ROWS // 128):
                at = i * ROWS + h * 128
                turned = jnp.transpose(acc[w, at:at + 128])
                dstat[w:w + 1, at:at + 128] = jnp.sum(turned, axis=0, keepdims=True)
    stat_copy = to_sibling(dstat, dstat_in, 1)
    stat_copy.start()

    def own_block(i, carry):
        rows = pl.ds(pl.multiple_of(i * ROWS, ROWS), ROWS)
        part = dot_t(zown[0], dose[rows, 0:width])
        for j in range(1, CHUNKS):
            part = part + dot_t(zown[j], dose[rows, j * width:(j + 1) * width])
        prod[0:genes, rows] = part
        return carry

    lax.fori_loop(0, blocks, own_block, 0)

    stat_copy.wait_recv()
    mean = (dstat[0:1, :] + dstat_in[0:1, :]) / donors
    var = (dstat[1:2, :] + dstat_in[1:2, :]) / donors - mean * mean
    rstd = lax.rsqrt(var + 1e-05)

    base = me * tiles

    def select(first, cis, sums_z, put):
        for t in range(tiles):
            cols = slice(t * TILE, (t + 1) * TILE)
            prod[first:first + genes, cols] = (
                prod[first:first + genes, cols] - mean[:, cols] * sums_z
            ) * rstd[:, cols]
        for k in range(2 * half_k):
            here = cis[:, k:k + 1] - base
            picked = jnp.zeros((genes, TILE), jnp.float32)
            for t in range(tiles):
                picked = jnp.where(
                    here == t, prod[first:first + genes, t * TILE:(t + 1) * TILE], picked
                )
            put(k // half_k, (k % half_k) * TILE, picked)

    def put_own(h, at, value):
        sel_own[h, :, at:at + TILE] = value

    select(0, cis_ref[...], z_sum, put_own)
    own_copy = to_sibling(sel_own.at[1 - core], own_in, 2)
    own_copy.start()

    z_sums = jnp.zeros((2 * genes, 1), jnp.float32)
    for j in range(CHUNKS):
        for side, there, _ in sides:
            @pl.when(there)
            def _():
                z_arrival(side, j).wait_recv()
        z_sums = z_sums + jnp.sum(zin[j].astype(jnp.float32), axis=1, keepdims=True)

        def nbr_block(i, carry):
            rows = pl.ds(pl.multiple_of(i * ROWS, ROWS), ROWS)
            part = dot_t(zin[j], dose[rows, j * width:(j + 1) * width])
            if j:
                part = part + prod[genes:3 * genes, rows]
            prod[genes:3 * genes, rows] = part
            return carry

        lax.fori_loop(0, blocks, nbr_block, 0)

    for side, there, _ in sides:
        @pl.when(there)
        def _():
            cis_arrival(side).wait_recv()

        def put_nbr(h, at, value):
            sel_nbr[h, side * genes:(side + 1) * genes, at:at + TILE] = value

        select((side + 1) * genes, cin[side], z_sums[side * genes:(side + 1) * genes], put_nbr)
    nbr_copy = to_sibling(sel_nbr.at[1 - core], nbr_in, 3)
    nbr_copy.start()
    nbr_copy.wait_recv()
    ret[...] = sel_nbr[core] + nbr_in[...]
    for side, there, _ in sides:
        @pl.when(there)
        def _():
            ret_copy(side).start()

    own_copy.wait_recv()
    corr_ref[...] = sel_own[core] + own_in[...]
    for side, there, _ in sides:
        @pl.when(there)
        def _():
            ret_arrival(side).wait_recv()
            corr_ref[...] += ret_in[side]
    correlation = corr_ref[...] / donors
    corr_ref[...] = correlation
    squared = jnp.minimum(correlation * correlation, 0.9)
    shape_a = (donors - 2) / 2.0
    pval_ref[...] = tail_probability(squared, shape_a, beta_log_constant(shape_a), CF_TERMS)

    for copy in (mom_copy, stat_copy, own_copy, nbr_copy):
        copy.wait_send()
    for side, there, _ in sides:
        @pl.when(there)
        def _():
            cis_copy(side).wait_send()
            ret_copy(side).wait_send()
            for j in range(CHUNKS):
                z_copy(side, j).wait_send()


def shards(dosage, expression, cis_tiles):
    variants, local = dosage.shape
    genes = expression.shape[0]
    cores = lax.axis_size("donor")
    regions = lax.axis_size("region")
    window = cis_tiles.shape[1]
    half = window * TILE // cores
    width = local // CHUNKS
    sizes = (genes, local, variants, regions, local * cores)
    f32, bf16 = jnp.float32, jnp.bfloat16
    dma = pltpu.SemaphoreType.DMA
    vmem = pl.BlockSpec(memory_space=pltpu.VMEM)
    return pl.pallas_call(
        functools.partial(kernel, sizes),
        out_shape=(
            jax.ShapeDtypeStruct((genes, half), f32),
            jax.ShapeDtypeStruct((genes, half), f32),
        ),
        in_specs=[pl.BlockSpec(memory_space=pl.ANY), vmem, vmem],
        out_specs=(vmem, vmem),
        scratch_shapes=[
            pltpu.VMEM((variants, local), bf16),
            pltpu.VMEM((CHUNKS, genes, width), bf16),
            pltpu.VMEM((CHUNKS, 2 * genes, width), bf16),
            pltpu.VMEM((2, genes, window), jnp.int32),
            pltpu.VMEM((genes, 128), f32),
            pltpu.VMEM((genes, 128), f32),
            pltpu.VMEM((2, variants, 128), f32),
            pltpu.VMEM((2, variants), f32),
            pltpu.VMEM((2, variants), f32),
            pltpu.VMEM((3 * genes, variants), f32),
            pltpu.VMEM((2, genes, half), f32),
            pltpu.VMEM((genes, half), f32),
            pltpu.VMEM((2, 2 * genes, half), f32),
            pltpu.VMEM((2 * genes, half), f32),
            pltpu.VMEM((2 * genes, half), f32),
            pltpu.VMEM((2, genes, half), f32),
            dma((variants // ROWS,)),
            dma((2, CHUNKS)),
            dma((2, CHUNKS)),
            dma((2,)),
            dma((2,)),
            dma((4,)),
            dma((4,)),
            dma((2,)),
            dma((2,)),
        ],
        compiler_params=pltpu.CompilerParams(
            collective_id=0, has_side_effects=True, vmem_limit_bytes=40 * 1024 * 1024
        ),
    )(dosage, expression, cis_tiles)


def solution(mesh):
    assert mesh.shape["donor"] == 2
    in_specs = (
        P(("grp", "region"), "donor"),
        P(("grp", "region"), "donor"),
        P(("grp", "region"), None),
    )
    out_specs = (P(("grp", "region"), "donor"), P(("grp", "region"), "donor"))
    return jax.shard_map(shards, mesh=mesh, in_specs=in_specs, out_specs=out_specs, check_vma=False)
```

time: 696 us -> 32.6 us (0.05)
  waiting for transfers between devices: 377 us -> 0 us
  local copies, waits for them, and re-layouts: 260 us -> 6.35 us
  Pallas kernels: 0 us -> 25.3 us
  other arithmetic: 21.9 us -> 0 us
  between operations: 14.2 us -> 0.64 us
  matrix products: 11.8 us -> 0 us
    ppermute x2 -> x0, waiting for transfers between devices: 359 us -> none  [the longest x1 356 us: with_halo(): before = lax.ppermute(last, axis, up)]
    gather x1 -> x0, local copies, waits for them, and re-layouts: 259 us -> none  [shards(): picked = jnp.take_along_axis(layered, index_grid, axis=1)]
    pallas_call x0 -> x1, Pallas kernels: none -> 25.3 us  [shards(): pl.pallas_call(functools.partial(kernel, sizes), out_shape=(jax.ShapeDtyp...]
    psum x1 -> x0, waiting for transfers between devices: 18.8 us -> none  [shards(): summed = lax.psum(partial_pairs, 'donor')]
    dot_general x1 -> x0, matrix products: 11.8 us -> none  [donor_product(): lax.dot_general(left_rows, right_rows, (((1,), (1,)), ((), ())), preferre...]
    convert_element_type x1 -> x0, other arithmetic: 11 us -> none  [scale_rows(): return ((values.astype(jnp.float32) - center[:, None]) * lax.rsqrt(spread...]
  transfers between devices with their start and end apart: 3 -> 0, of which waited for: 3 -> 0; matrix products, arithmetic and copies ran while one was open for 0% -> 0% of each run, Pallas kernels for 0% -> 0%
where the time goes in v1:
time: 32.6 us; the launch traced here: 32.3 us
  Pallas kernels  25.3 us (78%)
  local copies, waits for them, and re-layouts  6.35 us (19%)
  between operations  0.64 us (2%)
    pallas_call x1, Pallas kernels, shards(): pl.pallas_call(functools.partial(kernel, sizes), out_shape=(jax.ShapeDtyp...  25.3 us
    unnamed x7, local copies, waits for them, and re-layouts  6.35 us

profile of v1, /device:TPU:9, one launch (start us, length us, event | category | flops | bytes accessed | tf_op | source)
XLA Modules:
  0.0 32.3 jit_solution(17160088615463758638)
XLA Ops:
  0.6 0.8 %copy.5.cis_ref = s32[32,8]{1,0:T(8,128)S(1)} copy(s32[32,8]{0,1:T(8,128)} %param.5) | data formatting | bytes 2048 | tf_op args[2]
  1.4 0.0 copy-start
  1.4 3.4 %copy-done = bf16[1024,4096]{1,0:T(8,128)(2,1)S(1)} copy-done((bf16[1024,4096]{1,0:T(8,128)(2,1)S(1)}, bf16[1024,4096]{1,0:T(8,128)(2,1)}, u32[]{:S(2)}) %copy-start) | copy-done | bytes 8388632
  4.8 0.0 copy-start.1
  4.8 0.9 %copy-done.1 = bf16[32,4096]{1,0:T(8,128)(2,1)S(1)} copy-done((bf16[32,4096]{1,0:T(8,128)(2,1)S(1)}, bf16[32,4096]{1,0:T(8,128)(2,1)}, u32[]{:S(2)}) %copy-start.1) | copy-done | bytes 262168
  5.7 25.3 %shard_map.50 = (f32[32,512]{1,0:T(8,128)S(1)}, f32[32,512]{1,0:T(8,128)S(1)}) custom-call(bf16[1024,4096]{1,0:T(8,128)(2,1)S(1)} %copy-done, bf16[32,4096]{1,0:T(8,128)(2,1)S(1)} %copy-done.1, s32[32,8]{1,0:T(8,128)S(1)} %copy.5.cis_ref), custom_call_target="tpu_custom_call" | custom-call | tf_op jit(solution)/shard_map/pallas_call | solution.py:320
  31.0 0.6 %copy.8 = f32[32,512]{1,0:T(8,128)} copy(f32[32,512]{1,0:T(8,128)S(1)} %get-tuple-element.4) | data formatting | bytes 131072
  31.7 0.6 %copy.9 = f32[32,512]{1,0:T(8,128)} copy(f32[32,512]{1,0:T(8,128)S(1)} %get-tuple-element.5) | data formatting | bytes 131072
Async XLA Ops:
  1.4 3.4 %copy-start = (bf16[1024,4096]{1,0:T(8,128)(2,1)S(1)}, bf16[1024,4096]{1,0:T(8,128)(2,1)}, u32[]{:S(2)}) copy-start(bf16[1024,4096]{1,0:T(8,128)(2,1)} %dose_hbm.1) | copy-start | bytes 25165828
  4.8 0.9 %copy-start.1 = (bf16[32,4096]{1,0:T(8,128)(2,1)S(1)}, bf16[32,4096]{1,0:T(8,128)(2,1)}, u32[]{:S(2)}) copy-start(bf16[32,4096]{1,0:T(8,128)(2,1)} %expr_ref.1) | copy-start | bytes 786436

commit v2 on v1

--- a/solution.py
+++ b/solution.py
@@ -66,11 +66,11 @@
 
 def kernel(
     sizes,
-    dose_hbm, expr_ref, cis_ref,
+    dose_hbm, expr_hbm, cis_t,
     corr_ref, pval_ref,
-    dose, zown, zin, cin, mom, mom_in, acc, dstat, dstat_in, prod,
+    dose, expr_ref, cis_ref, zown, zin, cin, mom, mom_in, mom_all, nbr_mom, acc, dstat, dstat_in, prod,
     sel_own, own_in, sel_nbr, nbr_in, ret, ret_in,
-    dose_sem, z_send, z_recv, c_send, c_recv, s_send, s_recv, r_send, r_recv,
+    dose_sem, expr_sem, z_send, z_recv, c_send, c_recv, m_send, m_recv, s_send, s_recv, r_send, r_recv,
 ):
     genes, local, variants, regions, donors = sizes
     tiles = variants // TILE
@@ -93,6 +93,8 @@
         def _():
             pl.semaphore_signal(barrier, inc=1, device_id=where, device_id_type=MESH)
 
+    expr_load = pltpu.make_async_copy(expr_hbm, expr_ref, expr_sem)
+    expr_load.start()
     blocks = variants // ROWS
     loads = [
         pltpu.make_async_copy(
@@ -103,6 +105,8 @@
     for load in loads:
         load.start()
 
+    cis_ref[...] = jnp.transpose(cis_t[...])
+    expr_load.wait()
     total, square = lane_sums(lambda j: expr_ref[:, j * 128:(j + 1) * 128], local, genes)
     total = jnp.sum(total, axis=1, keepdims=True)
     square = jnp.sum(square, axis=1, keepdims=True)
@@ -113,6 +117,7 @@
         def _():
             zin[:, pl.ds(side * genes, genes), :] = jnp.zeros((CHUNKS, genes, width), jnp.bfloat16)
             cin[side] = jnp.zeros(cis_ref.shape, jnp.int32)
+            nbr_mom[side] = jnp.zeros((genes, 128), jnp.float32)
 
     pl.semaphore_wait(barrier, 1 + has_prev.astype(jnp.int32) + has_next.astype(jnp.int32))
 
@@ -122,9 +127,6 @@
             device_id=sibling, device_id_type=MESH,
         )
 
-    mom_copy = to_sibling(mom, mom_in, 0)
-    mom_copy.start()
-
     def cis_copy(side):
         return pltpu.make_async_remote_copy(
             src_ref=cis_ref, dst_ref=cin.at[1 - side], send_sem=c_send.at[side],
@@ -133,14 +135,14 @@
 
     def z_copy(side, j):
         return pltpu.make_async_remote_copy(
-            src_ref=zown.at[j], dst_ref=zin.at[j, pl.ds((1 - side) * genes, genes)],
+            src_ref=expr_hbm.at[:, pl.ds(j * width, width)], dst_ref=zin.at[j, pl.ds((1 - side) * genes, genes)],
             send_sem=z_send.at[side, j], recv_sem=z_recv.at[1 - side, j],
             device_id=sides[side][2], device_id_type=MESH,
         )
 
     def z_arrival(side, j):
         return pltpu.make_async_remote_copy(
-            src_ref=zown.at[j], dst_ref=zin.at[j, pl.ds(side * genes, genes)],
+            src_ref=expr_hbm.at[:, pl.ds(j * width, width)], dst_ref=zin.at[j, pl.ds(side * genes, genes)],
             send_sem=z_send.at[side, j], recv_sem=z_recv.at[side, j],
             device_id=sides[side][2], device_id_type=MESH,
         )
@@ -149,6 +151,18 @@
         return pltpu.make_async_remote_copy(
             src_ref=cis_ref, dst_ref=cin.at[side], send_sem=c_send.at[side],
             recv_sem=c_recv.at[side], device_id=sides[side][2], device_id_type=MESH,
+        )
+
+    def mom_out(side):
+        return pltpu.make_async_remote_copy(
+            src_ref=mom_all, dst_ref=nbr_mom.at[1 - side], send_sem=m_send.at[side],
+            recv_sem=m_recv.at[1 - side], device_id=sides[side][2], device_id_type=MESH,
+        )
+
+    def mom_arrival(side):
+        return pltpu.make_async_remote_copy(
+            src_ref=mom_all, dst_ref=nbr_mom.at[side], send_sem=m_send.at[side],
+            recv_sem=m_recv.at[side], device_id=sides[side][2], device_id_type=MESH,
         )
 
     def ret_copy(side):
@@ -165,27 +179,23 @@
             device_id=sides[side][2], device_id_type=MESH,
         )
 
-    mom_copy.wait_recv()
-    sums = mom[...] + mom_in[...]
-    center = sums[:, 0:1] / donors
-    spread = sums[:, 1:2] / donors - center * center
-    scale = lax.rsqrt(spread + 1e-05)
+    mom_copy = to_sibling(mom, mom_in, 0)
+    mom_copy.start()
+    for side, there, _ in sides:
+        @pl.when(there)
+        def _():
+            cis_copy(side).start()
+            for j in range(CHUNKS):
+                z_copy(side, j).start()
+
+    def standard(y, sums):
+        center = sums[:, 0:1] / donors
+        spread = sums[:, 1:2] / donors - center * center
+        scale = lax.rsqrt(spread + 1e-05)
+        return ((y.astype(jnp.float32) - center) * scale).astype(jnp.bfloat16)
+
+    group = 32
     z_sum = jnp.zeros((genes, 1), jnp.float32)
-    for j in range(CHUNKS):
-        y = expr_ref[:, j * width:(j + 1) * width].astype(jnp.float32)
-        z = ((y - center) * scale).astype(jnp.bfloat16)
-        zown[j] = z
-        for side, there, _ in sides:
-            @pl.when(there)
-            def _():
-                z_copy(side, j).start()
-        z_sum = z_sum + jnp.sum(z.astype(jnp.float32), axis=1, keepdims=True)
-    for side, there, _ in sides:
-        @pl.when(there)
-        def _():
-            cis_copy(side).start()
-
-    group = 32
     for i in range(blocks):
         loads[i].wait()
 
@@ -203,6 +213,17 @@
                 at = i * ROWS + h * 128
                 turned = jnp.transpose(acc[w, at:at + 128])
                 dstat[w:w + 1, at:at + 128] = jnp.sum(turned, axis=0, keepdims=True)
+        if i == blocks // 2 - 1:
+            mom_copy.wait_recv()
+            mom_all[...] = mom[...] + mom_in[...]
+            for side, there, _ in sides:
+                @pl.when(there)
+                def _():
+                    mom_out(side).start()
+            for j in range(CHUNKS):
+                z = standard(expr_ref[:, j * width:(j + 1) * width], mom_all[...])
+                zown[j] = z
+                z_sum = z_sum + jnp.sum(z.astype(jnp.float32), axis=1, keepdims=True)
     stat_copy = to_sibling(dstat, dstat_in, 1)
     stat_copy.start()
 
@@ -246,12 +267,20 @@
     own_copy.start()
 
     z_sums = jnp.zeros((2 * genes, 1), jnp.float32)
+    for side, there, _ in sides:
+        @pl.when(there)
+        def _():
+            cis_arrival(side).wait_recv()
+            mom_arrival(side).wait_recv()
+    nbr_sums = nbr_mom[...].reshape(2 * genes, 128)
     for j in range(CHUNKS):
         for side, there, _ in sides:
             @pl.when(there)
             def _():
                 z_arrival(side, j).wait_recv()
-        z_sums = z_sums + jnp.sum(zin[j].astype(jnp.float32), axis=1, keepdims=True)
+        z = standard(zin[j], nbr_sums)
+        zin[j] = z
+        z_sums = z_sums + jnp.sum(z.astype(jnp.float32), axis=1, keepdims=True)
 
         def nbr_block(i, carry):
             rows = pl.ds(pl.multiple_of(i * ROWS, ROWS), ROWS)
@@ -263,11 +292,7 @@
 
         lax.fori_loop(0, blocks, nbr_block, 0)
 
-    for side, there, _ in sides:
-        @pl.when(there)
-        def _():
-            cis_arrival(side).wait_recv()
-
+    for side in range(2):
         def put_nbr(h, at, value):
             sel_nbr[h, side * genes:(side + 1) * genes, at:at + TILE] = value
 
@@ -300,6 +325,7 @@
         @pl.when(there)
         def _():
             cis_copy(side).wait_send()
+            mom_out(side).wait_send()
             ret_copy(side).wait_send()
             for j in range(CHUNKS):
                 z_copy(side, j).wait_send()
@@ -317,21 +343,26 @@
     f32, bf16 = jnp.float32, jnp.bfloat16
     dma = pltpu.SemaphoreType.DMA
     vmem = pl.BlockSpec(memory_space=pltpu.VMEM)
+    hbm = pl.BlockSpec(memory_space=pltpu.HBM)
     return pl.pallas_call(
         functools.partial(kernel, sizes),
         out_shape=(
             jax.ShapeDtypeStruct((genes, half), f32),
             jax.ShapeDtypeStruct((genes, half), f32),
         ),
-        in_specs=[pl.BlockSpec(memory_space=pl.ANY), vmem, vmem],
+        in_specs=[hbm, hbm, vmem],
         out_specs=(vmem, vmem),
         scratch_shapes=[
             pltpu.VMEM((variants, local), bf16),
+            pltpu.VMEM((genes, local), bf16),
+            pltpu.VMEM((genes, window), jnp.int32),
             pltpu.VMEM((CHUNKS, genes, width), bf16),
             pltpu.VMEM((CHUNKS, 2 * genes, width), bf16),
             pltpu.VMEM((2, genes, window), jnp.int32),
             pltpu.VMEM((genes, 128), f32),
             pltpu.VMEM((genes, 128), f32),
+            pltpu.VMEM((genes, 128), f32),
+            pltpu.VMEM((2, genes, 128), f32),
             pltpu.VMEM((2, variants, 128), f32),
             pltpu.VMEM((2, variants), f32),
             pltpu.VMEM((2, variants), f32),
@@ -343,8 +374,11 @@
             pltpu.VMEM((2 * genes, half), f32),
             pltpu.VMEM((2, genes, half), f32),
             dma((variants // ROWS,)),
+            dma,
             dma((2, CHUNKS)),
             dma((2, CHUNKS)),
+            dma((2,)),
+            dma((2,)),
             dma((2,)),
             dma((2,)),
             dma((4,)),
@@ -355,7 +389,7 @@
         compiler_params=pltpu.CompilerParams(
             collective_id=0, has_side_effects=True, vmem_limit_bytes=40 * 1024 * 1024
         ),
-    )(dosage, expression, cis_tiles)
+    )(dosage, expression, cis_tiles.T)
 
 
 def solution(mesh):

time: 32.6 us -> 36.1 us (1.11)
  the two profiles are of different devices: /device:TPU:9 before, /device:TPU:23 now
where the time goes in v2:
time: 36.1 us; the launch traced here: 35.9 us
  Pallas kernels  29 us (80%)
  local copies, waits for them, and re-layouts  6.27 us (17%)
  between operations  0.65 us (2%)
    pallas_call x1, Pallas kernels, shards(): pl.pallas_call(functools.partial(kernel, sizes), out_shape=(jax.ShapeDtyp...  29 us
    unnamed x8, local copies, waits for them, and re-layouts  6.27 us

profile of v2, /device:TPU:23, one launch (start us, length us, event | category | flops | bytes accessed | tf_op | source)
XLA Modules:
  0.0 35.9 jit_solution(6014352982321247420)
XLA Ops:
  0.6 0.0 copy-start
  0.6 3.4 %copy-done = bf16[1024,4096]{1,0:T(8,128)(2,1)S(1)} copy-done((bf16[1024,4096]{1,0:T(8,128)(2,1)S(1)}, bf16[1024,4096]{1,0:T(8,128)(2,1)}, u32[]{:S(2)}) %copy-start) | copy-done | bytes 8388632
  4.0 0.0 copy-start.1
  4.0 0.9 %copy-done.1 = bf16[32,4096]{1,0:T(8,128)(2,1)S(1)} copy-done((bf16[32,4096]{1,0:T(8,128)(2,1)S(1)}, bf16[32,4096]{1,0:T(8,128)(2,1)}, u32[]{:S(2)}) %copy-start.1) | copy-done | bytes 262168
  5.0 0.0 copy-start.2
  5.0 0.7 %copy-done.2 = s32[32,8]{0,1:T(8,128)S(1)} copy-done((s32[32,8]{0,1:T(8,128)S(1)}, s32[32,8]{0,1:T(8,128)}, u32[]{:S(2)}) %copy-start.2) | copy-done | bytes 1048
  5.7 29.0 %shard_map.50 = (f32[32,512]{1,0:T(8,128)S(1)}, f32[32,512]{1,0:T(8,128)S(1)}) custom-call(bf16[1024,4096]{1,0:T(8,128)(2,1)S(1)} %copy-done, bf16[32,4096]{1,0:T(8,128)(2,1)S(1)} %copy-done.1, s32[8,32]{1,0:T(8,128)S(1)} %bitcast.1), custom_call_target="tpu_custom_call" | custom-call | tf_op jit(solution)/shard_map/pallas_call | solution.py:347
  34.6 0.6 %copy.7 = f32[32,512]{1,0:T(8,128)} copy(f32[32,512]{1,0:T(8,128)S(1)} %get-tuple-element.4) | data formatting | bytes 131072
  35.2 0.6 %copy.8 = f32[32,512]{1,0:T(8,128)} copy(f32[32,512]{1,0:T(8,128)S(1)} %get-tuple-element.5) | data formatting | bytes 131072
Async XLA Ops:
  0.6 3.4 %copy-start = (bf16[1024,4096]{1,0:T(8,128)(2,1)S(1)}, bf16[1024,4096]{1,0:T(8,128)(2,1)}, u32[]{:S(2)}) copy-start(bf16[1024,4096]{1,0:T(8,128)(2,1)} %dose_hbm.1) | copy-start | bytes 25165828
  4.0 0.9 %copy-start.1 = (bf16[32,4096]{1,0:T(8,128)(2,1)S(1)}, bf16[32,4096]{1,0:T(8,128)(2,1)}, u32[]{:S(2)}) copy-start(bf16[32,4096]{1,0:T(8,128)(2,1)} %expr_hbm.1) | copy-start | bytes 786436
  5.0 0.7 %copy-start.2 = (s32[32,8]{0,1:T(8,128)S(1)}, s32[32,8]{0,1:T(8,128)}, u32[]{:S(2)}) copy-start(s32[32,8]{0,1:T(8,128)} %param.5) | copy-start | bytes 3076

commit v3 on v1

--- a/solution.py
+++ b/solution.py
@@ -66,11 +66,11 @@
 
 def kernel(
     sizes,
-    dose_hbm, expr_ref, cis_ref,
+    dose_hbm, expr_hbm, cis_t,
     corr_ref, pval_ref,
-    dose, zown, zin, cin, mom, mom_in, acc, dstat, dstat_in, prod,
+    dose, expr_ref, cis_ref, zown, zin, cin, mom, mom_in, acc, dstat, dstat_in, prod,
     sel_own, own_in, sel_nbr, nbr_in, ret, ret_in,
-    dose_sem, z_send, z_recv, c_send, c_recv, s_send, s_recv, r_send, r_recv,
+    dose_sem, expr_sem, z_send, f_send, z_recv, c_send, c_recv, s_send, s_recv, r_send, r_recv,
 ):
     genes, local, variants, regions, donors = sizes
     tiles = variants // TILE
@@ -93,6 +93,22 @@
         def _():
             pl.semaphore_signal(barrier, inc=1, device_id=where, device_id_type=MESH)
 
+    odd = lax.rem(me, 2)
+    far_slot, near_slot = odd, 1 - odd
+    partner, ahead, behind = me + 1 - 2 * odd, me + 2 - 4 * odd, me - 2 + 4 * odd
+    has_ahead = jnp.logical_and(ahead >= 0, ahead < regions)
+    has_far = jnp.logical_and(behind >= 0, behind < regions)
+    ahead = jnp.clip(ahead, 0, regions - 1)
+    behind = jnp.clip(behind, 0, regions - 1)
+    for there, where in ((has_ahead, ahead), (has_far, behind)):
+        @pl.when(there)
+        def _():
+            pl.semaphore_signal(
+                barrier, inc=1, device_id={"region": where}, device_id_type=MESH
+            )
+
+    expr_load = pltpu.make_async_copy(expr_hbm, expr_ref, expr_sem)
+    expr_load.start()
     blocks = variants // ROWS
     loads = [
         pltpu.make_async_copy(
@@ -103,18 +119,22 @@
     for load in loads:
         load.start()
 
+    cis_ref[...] = jnp.transpose(cis_t[...])
+    expr_load.wait()
     total, square = lane_sums(lambda j: expr_ref[:, j * 128:(j + 1) * 128], local, genes)
     total = jnp.sum(total, axis=1, keepdims=True)
     square = jnp.sum(square, axis=1, keepdims=True)
     lane = lax.broadcasted_iota(jnp.int32, (genes, 128), 1)
     mom[...] = jnp.where(lane == 0, total, square)
-    for side in range(2):
-        @pl.when(jnp.logical_not(sides[side][1]))
-        def _():
-            zin[:, pl.ds(side * genes, genes), :] = jnp.zeros((CHUNKS, genes, width), jnp.bfloat16)
-            cin[side] = jnp.zeros(cis_ref.shape, jnp.int32)
-
-    pl.semaphore_wait(barrier, 1 + has_prev.astype(jnp.int32) + has_next.astype(jnp.int32))
+    @pl.when(jnp.logical_not(has_far))
+    def _():
+        zin[:, far_slot] = jnp.zeros((CHUNKS, genes, width), jnp.bfloat16)
+        cin[far_slot] = jnp.zeros(cis_ref.shape, jnp.int32)
+
+    greeted = 1
+    for there in (has_prev, has_next, has_ahead, has_far):
+        greeted = greeted + there.astype(jnp.int32)
+    pl.semaphore_wait(barrier, greeted)
 
     def to_sibling(src, dst, slot):
         return pltpu.make_async_remote_copy(
@@ -131,19 +151,31 @@
             recv_sem=c_recv.at[1 - side], device_id=sides[side][2], device_id_type=MESH,
         )
 
-    def z_copy(side, j):
-        return pltpu.make_async_remote_copy(
-            src_ref=zown.at[j], dst_ref=zin.at[j, pl.ds((1 - side) * genes, genes)],
-            send_sem=z_send.at[side, j], recv_sem=z_recv.at[1 - side, j],
-            device_id=sides[side][2], device_id_type=MESH,
-        )
-
-    def z_arrival(side, j):
-        return pltpu.make_async_remote_copy(
-            src_ref=zown.at[j], dst_ref=zin.at[j, pl.ds(side * genes, genes)],
-            send_sem=z_send.at[side, j], recv_sem=z_recv.at[side, j],
-            device_id=sides[side][2], device_id_type=MESH,
-        )
+    def z_copy(j):
+        return pltpu.make_async_remote_copy(
+            src_ref=zown.at[j], dst_ref=zin.at[j, far_slot], send_sem=z_send.at[j],
+            recv_sem=z_recv.at[far_slot, j], device_id={"region": partner}, device_id_type=MESH,
+        )
+
+    def z_onward(j):
+        return pltpu.make_async_remote_copy(
+            src_ref=zin.at[j, near_slot], dst_ref=zin.at[j, far_slot], send_sem=f_send.at[j],
+            recv_sem=z_recv.at[far_slot, j], device_id={"region": ahead}, device_id_type=MESH,
+        )
+
+    def z_near(j):
+        return pltpu.make_async_remote_copy(
+            src_ref=zown.at[j], dst_ref=zin.at[j, near_slot], send_sem=z_send.at[j],
+            recv_sem=z_recv.at[near_slot, j], device_id={"region": partner}, device_id_type=MESH,
+        )
+
+    def pass_on(chunks):
+        for j in chunks:
+            z_near(j).wait_recv()
+
+            @pl.when(has_ahead)
+            def _():
+                z_onward(j).start()
 
     def cis_arrival(side):
         return pltpu.make_async_remote_copy(
@@ -165,27 +197,13 @@
             device_id=sides[side][2], device_id_type=MESH,
         )
 
-    mom_copy.wait_recv()
-    sums = mom[...] + mom_in[...]
-    center = sums[:, 0:1] / donors
-    spread = sums[:, 1:2] / donors - center * center
-    scale = lax.rsqrt(spread + 1e-05)
+    for side, there, _ in sides:
+        @pl.when(there)
+        def _():
+            cis_copy(side).start()
+
+    group = 32
     z_sum = jnp.zeros((genes, 1), jnp.float32)
-    for j in range(CHUNKS):
-        y = expr_ref[:, j * width:(j + 1) * width].astype(jnp.float32)
-        z = ((y - center) * scale).astype(jnp.bfloat16)
-        zown[j] = z
-        for side, there, _ in sides:
-            @pl.when(there)
-            def _():
-                z_copy(side, j).start()
-        z_sum = z_sum + jnp.sum(z.astype(jnp.float32), axis=1, keepdims=True)
-    for side, there, _ in sides:
-        @pl.when(there)
-        def _():
-            cis_copy(side).start()
-
-    group = 32
     for i in range(blocks):
         loads[i].wait()
 
@@ -198,6 +216,18 @@
             return carry
 
         lax.fori_loop(0, ROWS // group, row_group, 0)
+        if i == 0:
+            mom_copy.wait_recv()
+            sums = mom[...] + mom_in[...]
+            center = sums[:, 0:1] / donors
+            spread = sums[:, 1:2] / donors - center * center
+            scale = lax.rsqrt(spread + 1e-05)
+            for j in range(CHUNKS):
+                y = expr_ref[:, j * width:(j + 1) * width].astype(jnp.float32)
+                z = ((y - center) * scale).astype(jnp.bfloat16)
+                zown[j] = z
+                z_copy(j).start()
+                z_sum = z_sum + jnp.sum(z.astype(jnp.float32), axis=1, keepdims=True)
         for w in range(2):
             for h in range(ROWS // 128):
                 at = i * ROWS + h * 128
@@ -214,7 +244,12 @@
         prod[0:genes, rows] = part
         return carry
 
-    lax.fori_loop(0, blocks, own_block, 0)
+    quarter = CHUNKS // 4
+    pass_on(range(quarter))
+    lax.fori_loop(0, blocks // 2, own_block, 0)
+    pass_on(range(quarter, 2 * quarter))
+    lax.fori_loop(blocks // 2, blocks, own_block, 0)
+    pass_on(range(2 * quarter, 3 * quarter))
 
     stat_copy.wait_recv()
     mean = (dstat[0:1, :] + dstat_in[0:1, :]) / donors
@@ -245,17 +280,19 @@
     own_copy = to_sibling(sel_own.at[1 - core], own_in, 2)
     own_copy.start()
 
+    pass_on(range(3 * quarter, CHUNKS))
     z_sums = jnp.zeros((2 * genes, 1), jnp.float32)
     for j in range(CHUNKS):
-        for side, there, _ in sides:
-            @pl.when(there)
-            def _():
-                z_arrival(side, j).wait_recv()
-        z_sums = z_sums + jnp.sum(zin[j].astype(jnp.float32), axis=1, keepdims=True)
+        @pl.when(has_far)
+        def _():
+            z_copy(j).wait_recv()
+
+        both = zin[j].reshape(2 * genes, width)
+        z_sums = z_sums + jnp.sum(both.astype(jnp.float32), axis=1, keepdims=True)
 
         def nbr_block(i, carry):
             rows = pl.ds(pl.multiple_of(i * ROWS, ROWS), ROWS)
-            part = dot_t(zin[j], dose[rows, j * width:(j + 1) * width])
+            part = dot_t(zin[j].reshape(2 * genes, width), dose[rows, j * width:(j + 1) * width])
             if j:
                 part = part + prod[genes:3 * genes, rows]
             prod[genes:3 * genes, rows] = part
@@ -301,8 +338,14 @@
         def _():
             cis_copy(side).wait_send()
             ret_copy(side).wait_send()
-            for j in range(CHUNKS):
-                z_copy(side, j).wait_send()
+
+    for j in range(CHUNKS):
+        z_copy(j).wait_send()
+
+    @pl.when(has_ahead)
+    def _():
+        for j in range(CHUNKS):
+            z_onward(j).wait_send()
 
 
 def shards(dosage, expression, cis_tiles):
@@ -317,18 +360,21 @@
     f32, bf16 = jnp.float32, jnp.bfloat16
     dma = pltpu.SemaphoreType.DMA
     vmem = pl.BlockSpec(memory_space=pltpu.VMEM)
+    hbm = pl.BlockSpec(memory_space=pltpu.HBM)
     return pl.pallas_call(
         functools.partial(kernel, sizes),
         out_shape=(
             jax.ShapeDtypeStruct((genes, half), f32),
             jax.ShapeDtypeStruct((genes, half), f32),
         ),
-        in_specs=[pl.BlockSpec(memory_space=pl.ANY), vmem, vmem],
+        in_specs=[hbm, hbm, vmem],
         out_specs=(vmem, vmem),
         scratch_shapes=[
             pltpu.VMEM((variants, local), bf16),
+            pltpu.VMEM((genes, local), bf16),
+            pltpu.VMEM((genes, window), jnp.int32),
             pltpu.VMEM((CHUNKS, genes, width), bf16),
-            pltpu.VMEM((CHUNKS, 2 * genes, width), bf16),
+            pltpu.VMEM((CHUNKS, 2, genes, width), bf16),
             pltpu.VMEM((2, genes, window), jnp.int32),
             pltpu.VMEM((genes, 128), f32),
             pltpu.VMEM((genes, 128), f32),
@@ -343,7 +389,9 @@
             pltpu.VMEM((2 * genes, half), f32),
             pltpu.VMEM((2, genes, half), f32),
             dma((variants // ROWS,)),
-            dma((2, CHUNKS)),
+            dma,
+            dma((CHUNKS,)),
+            dma((CHUNKS,)),
             dma((2, CHUNKS)),
             dma((2,)),
             dma((2,)),
@@ -353,13 +401,13 @@
             dma((2,)),
         ],
         compiler_params=pltpu.CompilerParams(
-            collective_id=0, has_side_effects=True, vmem_limit_bytes=40 * 1024 * 1024
+            collective_id=0, has_side_effects=True, vmem_limit_bytes=60 * 1024 * 1024
         ),
-    )(dosage, expression, cis_tiles)
+    )(dosage, expression, cis_tiles.T)
 
 
 def solution(mesh):
-    assert mesh.shape["donor"] == 2
+    assert mesh.shape["donor"] == 2 and mesh.shape["region"] % 2 == 0
     in_specs = (
         P(("grp", "region"), "donor"),
         P(("grp", "region"), "donor"),

time: 32.6 us -> 30.8 us (0.945)
  local copies, waits for them, and re-layouts: 6.35 us -> 2.95 us
  Pallas kernels: 25.3 us -> 27 us
    unnamed x7 -> x2, local copies, waits for them, and re-layouts: 6.35 us -> 2.95 us
    pallas_call x1, Pallas kernels: 25.3 us -> 27 us  [shards(): pl.pallas_call(functools.partial(kernel, sizes), out_shape=(jax.ShapeDtyp...]
where the time goes in v3:
time: 30.8 us; the launch traced here: 30.6 us
  Pallas kernels  27 us (88%)
  local copies, waits for them, and re-layouts  2.95 us (10%)
  between operations  0.64 us (2%)
    pallas_call x1, Pallas kernels, shards(): pl.pallas_call(functools.partial(kernel, sizes), out_shape=(jax.ShapeDtyp...  27 us
    unnamed x2, local copies, waits for them, and re-layouts  2.95 us

profile of v3, /device:TPU:9, one launch (start us, length us, event | category | flops | bytes accessed | tf_op | source)
XLA Modules:
  0.0 30.6 jit_solution(7050022195503015071)
XLA Ops:
  0.6 27.0 %shard_map.50 = (f32[32,512]{1,0:T(8,128)}, f32[32,512]{1,0:T(8,128)}) custom-call(bf16[1024,4096]{1,0:T(8,128)(2,1)} %dose_hbm.1, bf16[32,4096]{1,0:T(8,128)(2,1)} %expr_hbm.1, s32[8,32]{1,0:T(8,128)} %bitcast.1), custom_call_target="tpu_custom_call" | custom-call | tf_op jit(solution)/shard_map/pallas_call | solution.py:364
  27.6 1.5 %copy.7 = f32[32,512]{1,0:T(8,128)} copy(f32[32,512]{1,0:T(8,128)} %get-tuple-element.4) | data formatting | bytes 131072
  29.1 1.5 %copy.8 = f32[32,512]{1,0:T(8,128)} copy(f32[32,512]{1,0:T(8,128)} %get-tuple-element.5) | data formatting | bytes 131072

commit v4 on v3

--- a/solution.py
+++ b/solution.py
@@ -11,7 +11,7 @@
 TILE = 128
 CF_TERMS = 32
 CHUNKS = 4
-ROWS = 256
+ROWS = 512
 MESH = pl.DeviceIdType.MESH
 
 

time: 30.8 us -> 29.5 us (0.958)
  Pallas kernels: 27 us -> 25.6 us
    pallas_call x1, Pallas kernels: 27 us -> 25.6 us  [shards(): pl.pallas_call(functools.partial(kernel, sizes), out_shape=(jax.ShapeDtyp...]
where the time goes in v4:
time: 29.5 us; the launch traced here: 29.2 us
  Pallas kernels  25.6 us (87%)
  local copies, waits for them, and re-layouts  2.95 us (10%)
  between operations  0.64 us (2%)
    pallas_call x1, Pallas kernels, shards(): pl.pallas_call(functools.partial(kernel, sizes), out_shape=(jax.ShapeDtyp...  25.6 us
    unnamed x2, local copies, waits for them, and re-layouts  2.95 us

profile of v4, /device:TPU:9, one launch (start us, length us, event | category | flops | bytes accessed | tf_op | source)
XLA Modules:
  0.0 29.2 jit_solution(9675228428688528292)
XLA Ops:
  0.6 25.6 %shard_map.50 = (f32[32,512]{1,0:T(8,128)}, f32[32,512]{1,0:T(8,128)}) custom-call(bf16[1024,4096]{1,0:T(8,128)(2,1)} %dose_hbm.1, bf16[32,4096]{1,0:T(8,128)(2,1)} %expr_hbm.1, s32[8,32]{1,0:T(8,128)} %bitcast.1), custom_call_target="tpu_custom_call" | custom-call | tf_op jit(solution)/shard_map/pallas_call | solution.py:364
  26.3 1.5 %copy.7 = f32[32,512]{1,0:T(8,128)} copy(f32[32,512]{1,0:T(8,128)} %get-tuple-element.4) | data formatting | bytes 131072
  27.7 1.5 %copy.8 = f32[32,512]{1,0:T(8,128)} copy(f32[32,512]{1,0:T(8,128)} %get-tuple-element.5) | data formatting | bytes 131072
